TPU v7x, 32 devices: a whole 2x2x4 slice. The times are simulated.
32 devices in a mesh: head: 2 (over x), ffn: 4 (over y, core), row: 4 (over z).
Axes of the slice: x: 2, y: 2, z: 4, core: 2. Of those that a mesh axis runs over, the one named last changes fastest.
Arguments:
- inputs: bfloat16 [16, 640, 1024], P(('ffn', 'row'), 'head'), may hold values from -6 to 6
- first_values: bfloat16 [16, 640, 1024], P(('ffn', 'row'), 'head'), may hold values from -6 to 6
- lengths: int32 [16], P(('ffn', 'row')), may hold values from 512 to 640, as said below
- gain_attn: float32 [1024], replicated, may hold values from 0.5 to 1.5
- w_qkv: bfloat16 [1024, 3072], replicated, may hold values from -0.1875 to 0.1875
- w_out: bfloat16 [1024, 1024], replicated, may hold values from -3 to 3
- gain_mlp: float32 [1024], replicated, may hold values from 0.5 to 1.5
- w_gate: bfloat16 [1024, 2816], P(None, 'ffn'), may hold values from -0.1875 to 0.1875
- w_up: bfloat16 [1024, 2816], P(None, 'ffn'), may hold values from -0.1875 to 0.1875
- w_down: bfloat16 [2816, 1024], P('ffn'), may hold values from -0.109375 to 0.109375
- cotangent: bfloat16 [16, 640, 1024], P(('ffn', 'row'), 'head'), may hold values from -6 to 6
Outputs:
- output: bfloat16 [16, 640, 1024], P(('ffn', 'row'), 'head')
- grad_inputs: float32 [16, 640, 1024], P(('ffn', 'row'), 'head')
- grad_first_values: bfloat16 [16, 640, 1024], P(('ffn', 'row'), 'head')
- grad_gain_attn: float32 [1024], replicated
- grad_w_qkv: float32 [1024, 3072], P(('ffn', 'row'), 'head')
- grad_w_out: float32 [1024, 1024], P('head', ('ffn', 'row'))
- grad_gain_mlp: float32 [1024], replicated
- grad_w_gate: float32 [1024, 2816], P(('head', 'row'), 'ffn')
- grad_w_up: float32 [1024, 2816], P(('head', 'row'), 'ffn')
- grad_w_down: float32 [2816, 1024], P('ffn', ('head', 'row'))
Inputs may be any that keep to these rules, and one draw needn't show every extreme that they name: `lengths`: one bucket in every draw is full.
All inputs are finite; a program needn't handle non-finite values.
Results may differ from a plain program's by a relative error of at most 0.02.
Values may be sent and summed in bfloat16 or wider, within the bound.
No kernel may reach another device: no remote copies, remote signals or barrier semaphores. Data moves between devices by JAX's collectives and lax.ppermute only.
A program may use at most 128 MiB of HBM per device.

v0:
```python
import jax
import jax.numpy as jnp
from jax import lax
from jax.sharding import PartitionSpec as P

HEADS = 16
HD = 64
eps = 1e-06


def rms_scale(values):
    return lax.rsqrt(jnp.mean(values * values, axis=-1, keepdims=True) + eps)


def inner_rows(left, right):
    return lax.dot_general(
        left, right, (((0,), (0,)), ((), ())), preferred_element_type=jnp.float32
    )


def against(left, right):
    return lax.dot_general(
        left, right, (((1,), (1,)), ((), ())), preferred_element_type=jnp.float32
    )


def rotary(length, head_size):
    half_size = head_size // 2
    inverse = jnp.exp(
        -jnp.log(10000.0) * jnp.arange(half_size, dtype=jnp.float32) * 2.0 / head_size
    )
    angles = jnp.arange(length, dtype=jnp.float32)[:, None] * inverse[None, :]
    return (jnp.cos(angles), jnp.sin(angles))


def rotate(vectors, cosine, sine, sign):
    half_size = vectors.shape[-1] // 2
    first_half = vectors[..., :half_size]
    second_half = vectors[..., half_size:]
    cos_rows = cosine[:, None, :]
    sin_rows = sign * sine[:, None, :]
    return jnp.concatenate(
        [
            first_half * cos_rows - second_half * sin_rows,
            second_half * cos_rows + first_half * sin_rows,
        ],
        axis=-1,
    )


def masked_scores(q_rows, keys, start, valid):
    block_rows = q_rows.shape[0]
    raw = jnp.einsum("qhe,khe->hqk", q_rows, keys, preferred_element_type=jnp.float32)
    columns = jnp.arange(keys.shape[0], dtype=jnp.int32)
    positions = start + jnp.arange(block_rows, dtype=jnp.int32)
    allowed = (columns[None, :] <= positions[:, None]) & (columns[None, :] < valid)
    return jnp.where(allowed[None], 0.125 * raw, -1e30)


def attend_forward(query, keys, mixed, valid, block_rows):
    count = query.shape[0] // block_rows

    def step(carry, index):
        start = index * block_rows
        q_rows = lax.dynamic_slice_in_dim(query, start, block_rows, 0)
        scores = masked_scores(q_rows, keys, start, valid)
        top = jnp.max(scores, axis=-1, keepdims=True)
        expo = jnp.exp(scores - top)
        total = jnp.sum(expo, axis=-1, keepdims=True)
        weights = expo / total
        result = jnp.einsum(
            "hqk,khe->qhe", weights.astype(jnp.bfloat16), mixed, preferred_element_type=jnp.float32
        )
        return (carry, (result.astype(jnp.bfloat16), top + jnp.log(total)))

    _, (outs, log_sums) = lax.scan(step, 0, jnp.arange(count, dtype=jnp.int32))
    return (outs.reshape(query.shape), log_sums)


def attend_backward(query, keys, mixed, valid, log_sums, grad_out, block_rows):
    count = query.shape[0] // block_rows
    zeros = jnp.zeros(keys.shape, jnp.float32)

    def step(carry, index):
        key_sum, value_sum = carry
        start = index * block_rows
        q_rows = lax.dynamic_slice_in_dim(query, start, block_rows, 0)
        g_rows = lax.dynamic_slice_in_dim(grad_out, start, block_rows, 0)
        scores = masked_scores(q_rows, keys, start, valid)
        weights = jnp.exp(scores - log_sums[index])
        grad_w = jnp.einsum("qhe,khe->hqk", g_rows, mixed, preferred_element_type=jnp.float32)
        delta = jnp.sum(weights * grad_w, axis=-1, keepdims=True)
        grad_s = (weights * (grad_w - delta)).astype(jnp.bfloat16)
        grad_q = 0.125 * jnp.einsum(
            "hqk,khe->qhe", grad_s, keys, preferred_element_type=jnp.float32
        )
        key_sum = key_sum + 0.125 * jnp.einsum(
            "hqk,qhe->khe", grad_s, q_rows, preferred_element_type=jnp.float32
        )
        value_sum = value_sum + jnp.einsum(
            "hqk,qhe->khe", weights.astype(jnp.bfloat16), g_rows, preferred_element_type=jnp.float32
        )
        return ((key_sum, value_sum), grad_q)

    (grad_keys, grad_mixed), grad_query = lax.scan(
        step, (zeros, zeros), jnp.arange(count, dtype=jnp.int32)
    )
    return (grad_query.reshape(query.shape), grad_keys, grad_mixed)


def on_device(
    inputs,
    first_values,
    lengths,
    gain_attn,
    w_qkv,
    w_out,
    gain_mlp,
    w_gate,
    w_up,
    w_down,
    cotangent,
):
    tok_rows = inputs.shape[1]
    groups = lax.axis_size("head")
    heads_here = HEADS // groups
    span_rows = tok_rows * groups
    block_rows = span_rows // max(1, span_rows // 512)
    head_pos = lax.axis_index("head")
    valid_len = lengths[0]
    packed_cols = heads_here * 3 * HD
    out_cols = heads_here * HD
    rows_in = inputs[0].astype(jnp.float32)
    scale_one = rms_scale(rows_in)
    normed = (rows_in * scale_one * gain_attn).astype(jnp.bfloat16)
    earlier = first_values[0]
    w_heads = lax.dynamic_slice_in_dim(w_qkv, head_pos * packed_cols, packed_cols, 1)
    out_heads = lax.dynamic_slice_in_dim(w_out, head_pos * out_cols, out_cols, 0)
    gathered = lax.all_gather(normed, "head", axis=0, tiled=True)
    packed = jnp.dot(gathered, w_heads, preferred_element_type=jnp.float32).astype(jnp.bfloat16)
    early = lax.all_to_all(earlier, "head", split_axis=1, concat_axis=0, tiled=True)
    packed = packed.reshape(span_rows, heads_here, 3, HD)
    cosine, sine = rotary(span_rows, HD)
    query = rotate(packed[:, :, 0].astype(jnp.float32), cosine, sine, 1.0).astype(jnp.bfloat16)
    keys = rotate(packed[:, :, 1].astype(jnp.float32), cosine, sine, 1.0).astype(jnp.bfloat16)
    early_heads = early.reshape(span_rows, heads_here, HD).astype(jnp.float32)
    mixed = (0.5 * (packed[:, :, 2].astype(jnp.float32) + early_heads)).astype(jnp.bfloat16)
    attended, log_sums = attend_forward(query, keys, mixed, valid_len, block_rows)
    attended_flat = attended.reshape(span_rows, out_cols)
    piece = attended_flat
    projected = lax.psum_scatter(
        jnp.dot(piece, out_heads, preferred_element_type=jnp.float32),
        "head",
        scatter_dimension=0,
        tiled=True,
    )
    hidden = rows_in + projected
    scale_two = rms_scale(hidden)
    normed_two = (hidden * scale_two * gain_mlp).astype(jnp.bfloat16)
    mlp_rows = lax.all_gather(normed_two, "ffn", axis=0, tiled=True)
    gate_rows = jnp.dot(mlp_rows, w_gate, preferred_element_type=jnp.float32)
    up_rows = jnp.dot(mlp_rows, w_up, preferred_element_type=jnp.float32)
    sigmoid_gate = jax.nn.sigmoid(gate_rows)
    silu_gate = gate_rows * sigmoid_gate
    active = (silu_gate * up_rows).astype(jnp.bfloat16)
    piece = active
    down_rows = lax.psum_scatter(
        jnp.dot(piece, w_down, preferred_element_type=jnp.float32).astype(jnp.bfloat16),
        "ffn",
        scatter_dimension=0,
        tiled=True,
    ).astype(jnp.float32)
    output = (hidden + down_rows).astype(jnp.bfloat16)[None]
    grad_y = cotangent[0].astype(jnp.float32)
    grad_rows = lax.all_gather(grad_y.astype(jnp.bfloat16), "ffn", axis=0, tiled=True)
    grad_active = against(grad_rows, w_down)
    down_part = inner_rows(active, grad_rows)
    grad_gate = (
        grad_active * up_rows * sigmoid_gate * (1.0 + gate_rows * (1.0 - sigmoid_gate))
    ).astype(jnp.bfloat16)
    grad_up = (grad_active * silu_gate).astype(jnp.bfloat16)
    gate_part = inner_rows(mlp_rows, grad_gate)
    up_part = inner_rows(mlp_rows, grad_up)
    grad_normed_two = lax.psum_scatter(
        (against(grad_gate, w_gate) + against(grad_up, w_up)).astype(jnp.bfloat16),
        "ffn",
        scatter_dimension=0,
        tiled=True,
    ).astype(jnp.float32)
    grad_gain_two = jnp.sum(grad_normed_two * hidden * scale_two, axis=0)
    weighted_two = grad_normed_two * gain_mlp
    cube_two = scale_two * scale_two * scale_two
    grad_hidden = (
        grad_y
        + scale_two * weighted_two
        - hidden * cube_two * jnp.mean(weighted_two * hidden, axis=-1, keepdims=True)
    )
    grad_proj = grad_hidden.astype(jnp.bfloat16)
    proj_rows = lax.all_gather(grad_proj, "head", axis=0, tiled=True)
    grad_att = against(proj_rows, out_heads).astype(jnp.bfloat16)
    wout_heads = inner_rows(attended_flat, proj_rows)
    grad_att = grad_att.reshape(span_rows, heads_here, HD)
    grad_query, grad_keys, grad_mixed = attend_backward(
        query, keys, mixed, valid_len, log_sums, grad_att, block_rows
    )
    grad_packed = jnp.stack(
        [
            rotate(grad_query, cosine, sine, -1.0),
            rotate(grad_keys, cosine, sine, -1.0),
            0.5 * grad_mixed,
        ],
        axis=2,
    )
    grad_packed = grad_packed.astype(jnp.bfloat16).reshape(span_rows, packed_cols)
    grad_early = (0.5 * grad_mixed).astype(jnp.bfloat16).reshape(span_rows, out_cols)
    piece = grad_packed
    grad_normed = lax.psum_scatter(
        against(piece, w_heads).astype(jnp.bfloat16), "head", scatter_dimension=0, tiled=True
    ).astype(jnp.float32)
    wqkv_heads = inner_rows(gathered, grad_packed)
    grad_first = lax.all_to_all(grad_early, "head", split_axis=0, concat_axis=1, tiled=True)
    grad_gain_one = jnp.sum(grad_normed * rows_in * scale_one, axis=0)
    weighted_one = grad_normed * gain_attn
    cube_one = scale_one * scale_one * scale_one
    grad_in = (
        grad_hidden
        + scale_one * weighted_one
        - rows_in * cube_one * jnp.mean(weighted_one * rows_in, axis=-1, keepdims=True)
    )
    sum_qkv, sum_out = (
        lax.psum_scatter(
            wqkv_heads.astype(jnp.bfloat16), ("ffn", "row"), scatter_dimension=0, tiled=True
        ).astype(jnp.float32),
        lax.psum_scatter(
            wout_heads.astype(jnp.bfloat16), ("ffn", "row"), scatter_dimension=1, tiled=True
        ).astype(jnp.float32),
    )
    sum_gate, sum_up, sum_down = (
        lax.psum_scatter(gate_part, ("head", "row"), scatter_dimension=0, tiled=True),
        lax.psum_scatter(up_part, ("head", "row"), scatter_dimension=0, tiled=True),
        lax.psum_scatter(down_part, ("head", "row"), scatter_dimension=1, tiled=True),
    )
    gains_one, gains_two = lax.psum((grad_gain_one, grad_gain_two), ("head", "ffn", "row"))
    return (
        output,
        grad_in[None],
        grad_first[None],
        gains_one,
        sum_qkv,
        sum_out,
        gains_two,
        sum_gate,
        sum_up,
        sum_down,
    )


def solution(mesh):
    in_specs = (
        P(("ffn", "row"), "head", None),
        P(("ffn", "row"), "head", None),
        P(("ffn", "row")),
        P(),
        P(),
        P(),
        P(),
        P(None, "ffn"),
        P(None, "ffn"),
        P("ffn", None),
        P(("ffn", "row"), "head", None),
    )
    out_specs = (
        P(("ffn", "row"), "head", None),
        P(("ffn", "row"), "head", None),
        P(("ffn", "row"), "head", None),
        P(),
        P(("ffn", "row"), "head"),
        P("head", ("ffn", "row")),
        P(),
        P(("head", "row"), "ffn"),
        P(("head", "row"), "ffn"),
        P("ffn", ("head", "row")),
    )
    return jax.shard_map(
        on_device, mesh=mesh, in_specs=in_specs, out_specs=out_specs, check_vma=False
    )
```

profile of v0, /device:TPU:0, one launch (start us, length us, event | category | flops | bytes accessed | tf_op | source)
XLA Modules:
  0.0 695.1 jit_solution(10302706006738696550)
XLA Ops:
  13.5 4.3 all-to-all-start
  20.5 12.6 %all-to-all-done = bf16[320,2,512]{2,0,1:T(8,128)(2,1)} async-done(((bf16[320,2,512]{2,0,1:T(8,128)(2,1)}), bf16[320,2,512]{2,0,1:T(8,128)(2,1)}, u32[]{:S(2)}, u32[]{:S(2)}) %all-to-all-start) | async-done | bytes 655392 | tf_op jit(solution)/shard_map/all_to_all | solution.py:141
  42.9 5.8 convolution_convert_fusion.2
  48.7 4.0 copy.60
  62.5 4.0 fusion.29
  69.7 38.2 %reduce-scatter.10.cloned.1.call-done = f32[320,1024]{1,0:T(8,128)} async-done(((f32[640,1024]{1,0:T(8,128)}), f32[320,1024]{1,0:T(8,128)}) %reduce-scatter.10.cloned.1.call-update) | async-done | bytes 1310736 | tf_op jit(solution)/shard_map/reduce_scatter | solution.py:151
  111.6 24.9 %all-gather.8.cloned.1.call-done = bf16[1280,1024]{1,0:T(8,128)(2,1)} async-done(((bf16[320,1024]{1,0:T(8,128)(2,1)}), bf16[1280,1024]{1,0:T(8,128)(2,1)}) %all-gather.8.cloned.1.call-update) | async-done | bytes 2621456 | tf_op jit(solution)/shard_map/all_gather | solution.py:160
  136.5 6.1 fusion.68
  142.7 3.8 fusion.67
  146.5 17.1 %all-gather.12.cloned.1.call-done = bf16[1,1280,1024]{2,1,0:T(8,128)(2,1)} async-done(((bf16[1,320,1024]{2,1,0:T(8,128)(2,1)}), bf16[1,1280,1024]{2,1,0:T(8,128)(2,1)}) %all-gather.12.cloned.1.call-update) | async-done | bytes 2621456 | tf_op jit(solution)/shard_map/all_gather | solution.py:175
  163.6 8.8 %multiply_convert_fusion.1 = (bf16[1280,704]{0,1:T(8,128)(2,1)S(1)}, bf16[1280,704]{0,1:T(8,128)(2,1)S(1)}, bf16[1280,704]{0,1:T(8,128)(2,1)}) fusion(f32[1280,704]{0,1:T(8,128)} %fusion.67, f32[1280,704]{0,1:T(8,128)} %fusion.68, bf16[704,1024]{1,0:T(8,128)(2,1)} %param.20, bf16[1,1280,1024]{2,1,0:T(8,128)(2,1)} %all-gather.12.cloned.1.call-done), kind=kOutput, calls=%fused_computation.14 | convolution fusion | flops 1859010560 | bytes 16678912 | tf_op jit(solution)/shard_map/dot_general | solution.py:22
  174.9 3.9 add_convert_fusion
  178.8 34.8 %reduce-scatter.14.cloned.1.call-done = bf16[320,1024]{1,0:T(8,128)(2,1)} async-done(((bf16[1280,1024]{1,0:T(8,128)(2,1)}), bf16[320,1024]{1,0:T(8,128)(2,1)}) %reduce-scatter.14.cloned.1.call-update) | async-done | bytes 655376 | tf_op jit(solution)/shard_map/reduce_scatter | solution.py:184
  217.4 24.1 %all-gather.10.cloned.1.call-done = bf16[640,1024]{1,0:T(8,128)(2,1)} async-done(((bf16[320,1024]{1,0:T(8,128)(2,1)}), bf16[640,1024]{1,0:T(8,128)(2,1)}) %all-gather.10.cloned.1.call-update) | async-done | bytes 1310736 | tf_op jit(solution)/shard_map/all_gather | solution.py:199
  244.0 12.6 %multiply_reduce_fusion = (f32[8,640]{1,0:T(8,128)S(1)}, f32[8,640,640]{1,2,0:T(8,128)}) fusion(f32[8,640,640]{1,2,0:T(8,128)} %copy-done.2, f32[8,640]{1,0:T(8,128)S(1)} %log_add_fusion, bf16[640,8,64]{0,2,1:T(8,128)(2,1)S(1)} %bitcast.112, f32[640,8,64]{0,2,1:T(8,128)S(1)} %copy-done.8, bf16[640,8,3,64]{0,3,2,1:T(8,128)(2,1)} %bitcast.108), kind=kOutput, calls=%fused_computation.1 | convolution fusion | flops 430566400 | bytes 28876800 | tf_op jit(solution)/shard_map/while/body/eval_jaxpr/qhe,khe->hqk/dot_general | solution.py:91
  256.6 6.6 multiply_convert_fusion
  263.3 3.3 fusion.24
  273.1 7.1 %fusion.26 = bf16[8,64,640]{2,1,0:T(8,128)(2,1)S(1)} fusion(bf16[640,8,64]{0,2,1:T(8,128)(2,1)S(1)} %bitcast.113, f32[8,640,640]{1,2,0:T(8,128)} %copy-done.2, f32[8,640]{1,0:T(8,128)S(1)} %log_add_fusion), kind=kOutput, calls=%fused_computation.49 | convolution fusion | flops 426639360 | bytes 14438400 | tf_op jit(solution)/shard_map/while/body/eval_jaxpr/hqk,qhe->khe/dot_general | solution.py:100
  282.5 5.4 fusion.15
  288.0 5.2 convolution_convert_fusion.1
  294.8 5.4 convolution_convert_fusion
  301.7 5.4 fusion.10
  308.6 5.4 fusion.71
  315.5 5.3 fusion.70
  323.9 12.2 %all_to_all.29 = bf16[2,320,512]{2,1,0:T(8,128)(2,1)S(1)} all-to-all(bf16[2,320,512]{2,1,0:T(8,128)(2,1)S(1)} %copy.70), channel_id=1, replica_groups=mesh['head'=2,'ffn'=4,'row'=4] {'head'}, dimensions={0} | all-to-all | bytes 1310720 | tf_op jit(solution)/shard_map/all_to_all | solution.py:221
  339.5 13.2 %reduce-scatter.16.cloned.1.call-done = bf16[320,1024]{1,0:T(8,128)(2,1)} async-done(((bf16[640,1024]{1,0:T(8,128)(2,1)}), bf16[320,1024]{1,0:T(8,128)(2,1)}) %reduce-scatter.16.cloned.1.call-update) | async-done | bytes 655376 | tf_op jit(solution)/shard_map/reduce_scatter | solution.py:217
  354.3 39.6 %all-reduce = (f32[1024]{0:T(1024)}, f32[1024]{0:T(1024)}) all-reduce(f32[1024]{0:T(1024)S(1)} %get-tuple-element.53, f32[1024]{0:T(1024)S(1)} %copy-done.37), channel_id=1, replica_groups=mesh['head'=2,'ffn'=4,'row'=4] {'head','ffn','row'}, use_global_device_ids=true, to_apply=%region_12.13 | all-reduce | flops 2048 | bytes 16384 | tf_op jit(solution)/shard_map/psum | solution.py:243
  394.0 4.1 fusion.32
  398.0 62.5 %reduce-scatter.18.cloned.1.call-done = bf16[64,1536]{1,0:T(8,128)(2,1)} async-done(((bf16[1024,1536]{1,0:T(8,128)(2,1)}), bf16[64,1536]{1,0:T(8,128)(2,1)}) %reduce-scatter.18.cloned.1.call-update) | async-done | bytes 196624 | tf_op jit(solution)/shard_map/reduce_scatter | solution.py:231
  462.2 74.0 %reduce-scatter.26.cloned.1.call-done = f32[704,128]{1,0:T(8,128)} async-done(((f32[704,1024]{1,0:T(8,128)}), f32[704,128]{1,0:T(8,128)}) %reduce-scatter.26.cloned.1.call-update) | async-done | bytes 360464 | tf_op jit(solution)/shard_map/reduce_scatter | solution.py:241
  536.3 75.9 %reduce-scatter.24.cloned.1.call-done = f32[128,704]{0,1:T(8,128)} async-done(((f32[1024,704]{0,1:T(8,128)}), f32[128,704]{0,1:T(8,128)}) %reduce-scatter.24.cloned.1.call-update) | async-done | bytes 360464 | tf_op jit(solution)/shard_map/reduce_scatter | solution.py:240
  612.1 76.0 %reduce-scatter.22.cloned.1.call-done = f32[128,704]{0,1:T(8,128)} async-done(((f32[1024,704]{0,1:T(8,128)}), f32[128,704]{0,1:T(8,128)}) %reduce-scatter.22.cloned.1.call-update) | async-done | bytes 360464 | tf_op jit(solution)/shard_map/reduce_scatter | solution.py:239
  (178 shorter events, 67.9 us)
Async XLA Ops:
  7.2 60.1 %copy-start = (bf16[1024,1024]{1,0:T(8,128)(2,1)S(1)}, bf16[1024,1024]{1,0:T(8,128)(2,1)}, u32[]{:S(2)}) copy-start(bf16[1024,1024]{1,0:T(8,128)(2,1)} %param.16) | copy-start | bytes 6291460
  7.2 35.7 %all-gather.6.cloned.1.call-start = ((), (), s32[]{:S(2)}) async-start(), calls=%async_computation.11 | async-start | bytes 1966080 | tf_op jit(solution)/shard_map/all_gather | solution.py:139
  13.5 19.6 %all-to-all-start = ((bf16[320,2,512]{2,0,1:T(8,128)(2,1)}), bf16[320,2,512]{2,0,1:T(8,128)(2,1)}, u32[]{:S(2)}, u32[]{:S(2)}) async-start(bf16[320,2,512]{2,0,1:T(8,128)(2,1)} %copy.61), calls=%async_computation | async-start | bytes 1310720 | tf_op jit(solution)/shard_map/all_to_all | solution.py:141
  17.8 90.2 %reduce-scatter.10.cloned.1.call-start = ((), (), s32[]{:S(2)}) async-start(), calls=%async_computation.12 | async-start | bytes 3932160 | tf_op jit(solution)/shard_map/reduce_scatter | solution.py:151
  69.6 40.1 %copy-start.27 = (f32[1024]{0:T(1024)S(1)}, f32[1024]{0:T(1024)}, u32[]{:S(2)}) copy-start(f32[1024]{0:T(1024)} %param.17) | copy-start | bytes 12292
  69.7 66.8 %all-gather.8.cloned.1.call-start = ((), (), s32[]{:S(2)}) async-start(), calls=%async_computation.13 | async-start | bytes 3276800 | tf_op jit(solution)/shard_map/all_gather | solution.py:160
  109.7 106.1 %copy-start.28 = (f32[320]{0:T(512)}, f32[320]{0:T(512)S(1)}, u32[]{:S(2)}) copy-start(f32[320]{0:T(512)S(1)} %get-tuple-element.91) | copy-start | bytes 3844
  109.7 106.1 %copy-start.33 = (f32[320]{0:T(512)}, f32[320]{0:T(512)S(1)}, u32[]{:S(2)}) copy-start(f32[320]{0:T(512)S(1)} %get-tuple-element.90) | copy-start | bytes 3844
  110.8 52.8 %all-gather.12.cloned.1.call-start = ((), (), s32[]{:S(2)}) async-start(), calls=%async_computation.23 | async-start | bytes 3276800 | tf_op jit(solution)/shard_map/all_gather | solution.py:175
  111.3 102.2 %reduce-scatter.14.cloned.1.call-start = ((), (), s32[]{:S(2)}) async-start(), calls=%async_computation.15 | async-start | bytes 3276800 | tf_op jit(solution)/shard_map/reduce_scatter | solution.py:184
  178.8 62.7 %all-gather.10.cloned.1.call-start = ((), (), s32[]{:S(2)}) async-start(), calls=%async_computation.16 | async-start | bytes 1966080 | tf_op jit(solution)/shard_map/all_gather | solution.py:199
  217.1 120.9 %reduce-scatter.20.cloned.1.call-start = ((), (), s32[]{:S(2)}) async-start(), calls=%async_computation.19 | async-start | bytes 1114112 | tf_op jit(solution)/shard_map/reduce_scatter | solution.py:234
  243.9 12.6 %copy-start.9 = (bf16[640,512]{0,1:T(8,128)(2,1)}, bf16[640,512]{0,1:T(8,128)(2,1)S(1)}, u32[]{:S(2)}) copy-start(bf16[640,512]{0,1:T(8,128)(2,1)S(1)} %convolution_convert_fusion.4) | copy-start | bytes 1966084
  243.9 12.6 %slice-start = ((s8[13107200]{0:T(1024)(128)(4,1)}), s8[4194304]{0:T(1024)(128)(4,1)S(1)}, s32[]{:S(2)}) async-start(s8[13107200]{0:T(1024)(128)(4,1)} %bitcast.104), calls=%async_computation.24 | async-start | bytes 8388608
  244.0 12.6 %slice-start.1 = ((s8[13107200]{0:T(1024)(128)(4,1)}), s8[4194304]{0:T(1024)(128)(4,1)S(1)}, s32[]{:S(2)}) async-start(s8[13107200]{0:T(1024)(128)(4,1)} %bitcast.104), calls=%async_computation.25 | async-start | bytes 8388608
  244.0 12.6 %slice-start.2 = ((s8[13107200]{0:T(1024)(128)(4,1)}), s8[4194304]{0:T(1024)(128)(4,1)S(1)}, s32[]{:S(2)}) async-start(s8[13107200]{0:T(1024)(128)(4,1)} %bitcast.104), calls=%async_computation.26 | async-start | bytes 8388608
  244.0 12.6 %slice-start.3 = ((s8[13107200]{0:T(1024)(128)(4,1)}), s8[524288]{0:T(1024)(128)(4,1)S(1)}, s32[]{:S(2)}) async-start(s8[13107200]{0:T(1024)(128)(4,1)} %bitcast.104), calls=%async_computation.27 | async-start | bytes 1048576
  270.1 82.7 %reduce-scatter.16.cloned.1.call-start = ((), (), s32[]{:S(2)}) async-start(), calls=%async_computation.17 | async-start | bytes 1966080 | tf_op jit(solution)/shard_map/reduce_scatter | solution.py:217
  288.0 106.0 %reduce-scatter.12.cloned.1.call-start = ((), (), s32[]{:S(2)}) async-start(), calls=%async_computation.14 | async-start | bytes 3276800 | tf_op jit(solution)/shard_map/reduce_scatter | solution.py:167
  293.3 167.3 %reduce-scatter.18.cloned.1.call-start = ((), (), s32[]{:S(2)}) async-start(), calls=%async_computation.18 | async-start | bytes 3342336 | tf_op jit(solution)/shard_map/reduce_scatter | solution.py:231
  300.2 236.0 %reduce-scatter.26.cloned.1.call-start = ((), (), s32[]{:S(2)}) async-start(), calls=%async_computation.22 | async-start | bytes 3244032 | tf_op jit(solution)/shard_map/reduce_scatter | solution.py:241
  307.1 305.0 %reduce-scatter.24.cloned.1.call-start = ((), (), s32[]{:S(2)}) async-start(), calls=%async_computation.21 | async-start | bytes 3244032 | tf_op jit(solution)/shard_map/reduce_scatter | solution.py:240
  314.1 374.0 %reduce-scatter.22.cloned.1.call-start = ((), (), s32[]{:S(2)}) async-start(), calls=%async_computation.20 | async-start | bytes 3244032 | tf_op jit(solution)/shard_map/reduce_scatter | solution.py:239
  323.8 28.9 %copy-start.3 = (bf16[1,320,1024]{2,1,0:T(8,128)(2,1)S(1)}, bf16[1,320,1024]{2,1,0:T(8,128)(2,1)}, u32[]{:S(2)}) copy-start(bf16[1,320,1024]{2,1,0:T(8,128)(2,1)} %param.11) | copy-start | bytes 1966084
  323.8 28.9 %copy-start.30 = (f32[1024]{0:T(1024)S(1)}, f32[1024]{0:T(1024)}, u32[]{:S(2)}) copy-start(f32[1024]{0:T(1024)} %param.14) | copy-start | bytes 12292
  323.8 28.9 %copy-start.32 = (f32[320]{0:T(512)S(1)}, f32[320]{0:T(512)}, u32[]{:S(2)}) copy-start(f32[320]{0:T(512)} %copy-done.31) | copy-start | bytes 3844
  336.0 18.3 %copy-start.37 = (f32[1024]{0:T(1024)S(1)}, f32[1024]{0:T(1024)}, u32[]{:S(2)}) copy-start(f32[1024]{0:T(1024)} %get-tuple-element.51) | copy-start | bytes 12292
  336.0 57.9 %copy-start.29 = (f32[320]{0:T(512)S(1)}, f32[320]{0:T(512)}, u32[]{:S(2)}) copy-start(f32[320]{0:T(512)} %copy-done.28) | copy-start | bytes 3844
  336.0 57.9 %copy-start.34 = (f32[320]{0:T(512)S(1)}, f32[320]{0:T(512)}, u32[]{:S(2)}) copy-start(f32[320]{0:T(512)} %copy-done.33) | copy-start | bytes 3844
  336.0 57.9 %copy-start.36 = (f32[320]{0:T(512)S(1)}, f32[320]{0:T(512)}, u32[]{:S(2)}) copy-start(f32[320]{0:T(512)} %copy-done.35) | copy-start | bytes 3844
  336.0 57.9 %copy-start.38 = (f32[320]{0:T(512)S(1)}, f32[320]{0:T(512)}, u32[]{:S(2)}) copy-start(f32[320]{0:T(512)} %get-tuple-element.88) | copy-start | bytes 3844
  394.0 294.1 %copy-start.1 = (bf16[1024,1024]{1,0:T(8,128)(2,1)S(1)}, bf16[1024,1024]{1,0:T(8,128)(2,1)}, u32[]{:S(2)}) copy-start(bf16[1024,1024]{1,0:T(8,128)(2,1)} %param.16) | copy-start | bytes 6291460
  (36 other events, 102.5 us)
Sparse Core Ops, SparseCore 0:
  12.2 30.6 all-gather.5
  69.8 38.1 reduce-scatter.9
  110.9 25.5 all-gather.7
  138.0 25.5 all-gather.11
  178.9 34.6 reduce-scatter.13
  217.2 24.2 all-gather.9
  270.2 57.4 reduce-scatter.19
  330.6 22.1 reduce-scatter.15
  355.3 34.8 reduce-scatter.11
  394.3 66.1 reduce-scatter.17
  465.1 71.1 reduce-scatter.25
  540.7 71.4 reduce-scatter.23
  616.7 71.3 reduce-scatter.21
where the time goes:
time: 706 us; the launch traced here: 695 us
  waiting for transfers between devices  457 us (65%)
  matrix products  100 us (14%)
  blocking collectives  51.8 us (7%)
  other arithmetic  34.9 us (5%)
  local copies, waits for them, and re-layouts  29.6 us (4%)
  between operations  15.7 us (2%)
    reduce_scatter x1, waiting for transfers between devices, on_device(): lax.psum_scatter(gate_part, ('head', 'row'), scatter_dimension=0, tiled=T...  76 us
    reduce_scatter x1, waiting for transfers between devices, on_device(): lax.psum_scatter(up_part, ('head', 'row'), scatter_dimension=0, tiled=True)  75.9 us
    reduce_scatter x1, waiting for transfers between devices, on_device(): lax.psum_scatter(down_part, ('head', 'row'), scatter_dimension=1, tiled=T...  74 us
    reduce_scatter x1, waiting for transfers between devices, on_device(): lax.psum_scatter(wqkv_heads.astype(jnp.bfloat16), ('ffn', 'row'), scatter...  62.5 us
    psum x1, blocking collectives, on_device(): lax.psum((grad_gain_one, grad_gain_two), ('head', 'ffn', 'row'))  39.6 us
    reduce_scatter x1, waiting for transfers between devices, on_device(): lax.psum_scatter(jnp.dot(piece, out_heads, preferred_element_type=jnp.flo...  38.2 us
    reduce_scatter x1, waiting for transfers between devices, on_device(): lax.psum_scatter((against(grad_gate, w_gate) + against(grad_up, w_up)).as...  34.8 us
    all_gather x1, waiting for transfers between devices, on_device(): mlp_rows = lax.all_gather(normed_two, 'ffn', axis=0, tiled=True)  24.9 us
  transfers between devices with their start and end apart: 14, of which 12 were waited for; matrix products, arithmetic and copies ran while one was open for 11% of the time, Pallas kernels for 0%

commit v1 on v0

--- a/solution.py
+++ b/solution.py
@@ -6,6 +6,19 @@
 HEADS = 16
 HD = 64
 eps = 1e-06
+
+
+def gather_around(value, axis, dim):
+    ways = lax.axis_size(axis)
+    up = [(d, (d + 1) % ways) for d in range(ways)]
+    down = [(d, (d - 1) % ways) for d in range(ways)]
+    earlier, later = ([value], [value])
+    for _ in range(ways // 2):
+        earlier.append(lax.ppermute(earlier[-1], axis, up))
+    for _ in range((ways - 1) // 2):
+        later.append(lax.ppermute(later[-1], axis, down))
+    line = jnp.concatenate([*earlier[::-1], *later[1:]], axis=dim)
+    return jnp.roll(line, (lax.axis_index(axis) - ways // 2) * value.shape[dim], axis=dim)
 
 
 def rms_scale(values):
@@ -172,7 +185,7 @@
     ).astype(jnp.float32)
     output = (hidden + down_rows).astype(jnp.bfloat16)[None]
     grad_y = cotangent[0].astype(jnp.float32)
-    grad_rows = lax.all_gather(grad_y.astype(jnp.bfloat16), "ffn", axis=0, tiled=True)
+    grad_rows = gather_around(grad_y.astype(jnp.bfloat16), "ffn", 0)
     grad_active = against(grad_rows, w_down)
     down_part = inner_rows(active, grad_rows)
     grad_gate = (

time: 706 us -> 710 us (level)
  local copies, waits for them, and re-layouts: 29.6 us -> 43.3 us
    ppermute x0 -> x3, waiting for transfers between devices: none -> 35 us  [the longest x2 35 us: gather_around(): earlier.append(lax.ppermute(earlier[-1], axis, up))]
    all_gather x1, waiting for transfers between devices: 24.9 us -> 0.01 us  [on_device(): mlp_rows = lax.all_gather(normed_two, 'ffn', axis=0, tiled=True)]
    all_gather x1 -> x0, waiting for transfers between devices: 17.1 us -> none  [on_device(): lax.all_gather(grad_y.astype(jnp.bfloat16), 'ffn', axis=0, tiled=True)]
    unnamed x108 -> x117, local copies, waits for them, and re-layouts: 14.9 us -> 26.7 us
  transfers between devices with their start and end apart: 14 -> 16, of which waited for: 12 -> 12; matrix products, arithmetic and copies ran while one was open for 11% -> 11% of each run, Pallas kernels for 0% -> 0%
where the time goes in v1:
time: 710 us; the launch traced here: 699 us
  waiting for transfers between devices  452 us (64%)
  matrix products  94.4 us (13%)
  blocking collectives  51.8 us (7%)
  local copies, waits for them, and re-layouts  43.3 us (6%)
  other arithmetic  34.9 us (5%)
  between operations  16 us (2%)
  starting transfers between devices  7.49 us (1%)
    reduce_scatter x1, waiting for transfers between devices, on_device(): lax.psum_scatter(up_part, ('head', 'row'), scatter_dimension=0, tiled=True)  76.1 us
    reduce_scatter x1, waiting for transfers between devices, on_device(): lax.psum_scatter(gate_part, ('head', 'row'), scatter_dimension=0, tiled=T...  76 us
    reduce_scatter x1, waiting for transfers between devices, on_device(): lax.psum_scatter(down_part, ('head', 'row'), scatter_dimension=1, tiled=T...  74 us
    reduce_scatter x1, waiting for transfers between devices, on_device(): lax.psum_scatter(wqkv_heads.astype(jnp.bfloat16), ('ffn', 'row'), scatter...  62.6 us
    psum x1, blocking collectives, on_device(): lax.psum((grad_gain_one, grad_gain_two), ('head', 'ffn', 'row'))  39.6 us
    reduce_scatter x1, waiting for transfers between devices, on_device(): lax.psum_scatter(jnp.dot(piece, out_heads, preferred_element_type=jnp.flo...  38.2 us
    reduce_scatter x1, waiting for transfers between devices, on_device(): lax.psum_scatter((against(grad_gate, w_gate) + against(grad_up, w_up)).as...  36.3 us
    ppermute x2, waiting for transfers between devices, gather_around(): earlier.append(lax.ppermute(earlier[-1], axis, up))  35 us
  transfers between devices with their start and end apart: 16, of which 12 were waited for; matrix products, arithmetic and copies ran while one was open for 11% of the time, Pallas kernels for 0%

profile of v1, /device:TPU:0, one launch (start us, length us, event | category | flops | bytes accessed | tf_op | source)
XLA Modules:
  0.0 699.5 jit_solution(9591232208006623306)
XLA Ops:
  13.5 4.3 all-to-all-start
  20.5 12.6 %all-to-all-done = bf16[320,2,512]{2,0,1:T(8,128)(2,1)} async-done(((bf16[320,2,512]{2,0,1:T(8,128)(2,1)}), bf16[320,2,512]{2,0,1:T(8,128)(2,1)}, u32[]{:S(2)}, u32[]{:S(2)}) %all-to-all-start) | async-done | bytes 655392 | tf_op jit(solution)/shard_map/all_to_all | solution.py:154
  39.7 3.2 all-gather.4.cloned.1.call-done
  42.9 5.8 convolution_convert_fusion.2
  48.7 4.0 copy.60
  62.4 4.0 fusion.29
  69.7 38.2 %reduce-scatter.10.cloned.1.call-done = f32[320,1024]{1,0:T(8,128)} async-done(((f32[640,1024]{1,0:T(8,128)}), f32[320,1024]{1,0:T(8,128)}) %reduce-scatter.10.cloned.1.call-update) | async-done | bytes 1310736 | tf_op jit(solution)/shard_map/reduce_scatter | solution.py:164
  110.8 10.4 %collective-permute-done = bf16[320,1024]{1,0:T(8,128)(2,1)} collective-permute-done((bf16[320,1024]{1,0:T(8,128)(2,1)}, bf16[320,1024]{1,0:T(8,128)(2,1)}, u32[]{:S(2)}, u32[]{:S(2)}) %collective-permute-start) | collective-permute-done | bytes 655392 | tf_op jit(solution)/shard_map/ppermute | solution.py:17
  123.2 24.6 %collective-permute-done.1 = bf16[320,1024]{1,0:T(8,128)(2,1)} collective-permute-done((bf16[320,1024]{1,0:T(8,128)(2,1)}, bf16[320,1024]{1,0:T(8,128)(2,1)}, u32[]{:S(2)}, u32[]{:S(2)}) %collective-permute-start.1) | collective-permute-done | bytes 655392 | tf_op jit(solution)/shard_map/ppermute | solution.py:17
  161.5 4.4 fusion.70
  168.0 6.6 multiply_convert_fusion.1
  177.0 3.9 add_convert_fusion
  181.0 36.3 %reduce-scatter.14.cloned.1.call-done = bf16[320,1024]{1,0:T(8,128)(2,1)} async-done(((bf16[1280,1024]{1,0:T(8,128)(2,1)}), bf16[320,1024]{1,0:T(8,128)(2,1)}) %reduce-scatter.14.cloned.1.call-update) | async-done | bytes 655376 | tf_op jit(solution)/shard_map/reduce_scatter | solution.py:197
  221.0 24.1 %all-gather.8.cloned.1.call-done = bf16[640,1024]{1,0:T(8,128)(2,1)} async-done(((bf16[320,1024]{1,0:T(8,128)(2,1)}), bf16[640,1024]{1,0:T(8,128)(2,1)}) %all-gather.8.cloned.1.call-update) | async-done | bytes 1310736 | tf_op jit(solution)/shard_map/all_gather | solution.py:212
  247.7 12.6 %multiply_reduce_fusion = (f32[8,640]{1,0:T(8,128)S(1)}, f32[8,640,640]{1,2,0:T(8,128)}) fusion(f32[8,640,640]{1,2,0:T(8,128)} %copy-done.2, f32[8,640]{1,0:T(8,128)S(1)} %log_add_fusion, bf16[640,8,64]{0,2,1:T(8,128)(2,1)S(1)} %bitcast.108, f32[640,8,64]{0,2,1:T(8,128)S(1)} %copy-done.9, bf16[640,8,3,64]{0,3,2,1:T(8,128)(2,1)} %bitcast.104), kind=kOutput, calls=%fused_computation.1 | convolution fusion | flops 430566400 | bytes 28876800 | tf_op jit(solution)/shard_map/while/body/eval_jaxpr/qhe,khe->hqk/dot_general | solution.py:104
  260.3 6.6 multiply_convert_fusion
  266.9 3.3 fusion.24
  276.8 7.1 %fusion.26 = bf16[8,64,640]{2,1,0:T(8,128)(2,1)S(1)} fusion(bf16[640,8,64]{0,2,1:T(8,128)(2,1)S(1)} %bitcast.109, f32[8,640,640]{1,2,0:T(8,128)} %copy-done.2, f32[8,640]{1,0:T(8,128)S(1)} %log_add_fusion), kind=kOutput, calls=%fused_computation.49 | convolution fusion | flops 426639360 | bytes 14438400 | tf_op jit(solution)/shard_map/while/body/eval_jaxpr/hqk,qhe->khe/dot_general | solution.py:113
  286.2 5.4 fusion.15
  291.7 5.2 convolution_convert_fusion.1
  298.5 5.4 convolution_convert_fusion
  305.3 5.4 fusion.10
  312.3 5.4 fusion.73
  319.2 5.3 fusion.72
  327.5 12.2 %all_to_all.29 = bf16[2,320,512]{2,1,0:T(8,128)(2,1)S(1)} all-to-all(bf16[2,320,512]{2,1,0:T(8,128)(2,1)S(1)} %copy.70), channel_id=1, replica_groups=mesh['head'=2,'ffn'=4,'row'=4] {'head'}, dimensions={0} | all-to-all | bytes 1310720 | tf_op jit(solution)/shard_map/all_to_all | solution.py:234
  343.2 13.2 %reduce-scatter.16.cloned.1.call-done = bf16[320,1024]{1,0:T(8,128)(2,1)} async-done(((bf16[640,1024]{1,0:T(8,128)(2,1)}), bf16[320,1024]{1,0:T(8,128)(2,1)}) %reduce-scatter.16.cloned.1.call-update) | async-done | bytes 655376 | tf_op jit(solution)/shard_map/reduce_scatter | solution.py:230
  358.0 39.6 %all-reduce = (f32[1024]{0:T(1024)}, f32[1024]{0:T(1024)}) all-reduce(f32[1024]{0:T(1024)S(1)} %get-tuple-element.53, f32[1024]{0:T(1024)S(1)} %copy-done.38), channel_id=1, replica_groups=mesh['head'=2,'ffn'=4,'row'=4] {'head','ffn','row'}, use_global_device_ids=true, to_apply=%region_12.13 | all-reduce | flops 2048 | bytes 16384 | tf_op jit(solution)/shard_map/psum | solution.py:256
  397.6 4.1 fusion.32
  401.7 62.6 %reduce-scatter.18.cloned.1.call-done = bf16[64,1536]{1,0:T(8,128)(2,1)} async-done(((bf16[1024,1536]{1,0:T(8,128)(2,1)}), bf16[64,1536]{1,0:T(8,128)(2,1)}) %reduce-scatter.18.cloned.1.call-update) | async-done | bytes 196624 | tf_op jit(solution)/shard_map/reduce_scatter | solution.py:244
  466.0 74.0 %reduce-scatter.26.cloned.1.call-done = f32[704,128]{1,0:T(8,128)} async-done(((f32[704,1024]{1,0:T(8,128)}), f32[704,128]{1,0:T(8,128)}) %reduce-scatter.26.cloned.1.call-update) | async-done | bytes 360464 | tf_op jit(solution)/shard_map/reduce_scatter | solution.py:254
  540.0 76.1 %reduce-scatter.24.cloned.1.call-done = f32[128,704]{0,1:T(8,128)} async-done(((f32[1024,704]{0,1:T(8,128)}), f32[128,704]{0,1:T(8,128)}) %reduce-scatter.24.cloned.1.call-update) | async-done | bytes 360464 | tf_op jit(solution)/shard_map/reduce_scatter | solution.py:253
  616.1 76.0 %reduce-scatter.22.cloned.1.call-done = f32[128,704]{0,1:T(8,128)} async-done(((f32[1024,704]{0,1:T(8,128)}), f32[128,704]{0,1:T(8,128)}) %reduce-scatter.22.cloned.1.call-update) | async-done | bytes 360464 | tf_op jit(solution)/shard_map/reduce_scatter | solution.py:252
  (191 shorter events, 81.7 us)
Async XLA Ops:
  7.2 60.0 %copy-start = (bf16[1024,1024]{1,0:T(8,128)(2,1)S(1)}, bf16[1024,1024]{1,0:T(8,128)(2,1)}, u32[]{:S(2)}) copy-start(bf16[1024,1024]{1,0:T(8,128)(2,1)} %param.16) | copy-start | bytes 6291460
  7.2 35.7 %all-gather.4.cloned.1.call-start = ((), (), s32[]{:S(2)}) async-start(), calls=%async_computation.11 | async-start | bytes 1966080 | tf_op jit(solution)/shard_map/all_gather | solution.py:152
  13.5 19.6 %all-to-all-start = ((bf16[320,2,512]{2,0,1:T(8,128)(2,1)}), bf16[320,2,512]{2,0,1:T(8,128)(2,1)}, u32[]{:S(2)}, u32[]{:S(2)}) async-start(bf16[320,2,512]{2,0,1:T(8,128)(2,1)} %copy.61), calls=%async_computation | async-start | bytes 1310720 | tf_op jit(solution)/shard_map/all_to_all | solution.py:154
  17.8 90.1 %reduce-scatter.10.cloned.1.call-start = ((), (), s32[]{:S(2)}) async-start(), calls=%async_computation.12 | async-start | bytes 3932160 | tf_op jit(solution)/shard_map/reduce_scatter | solution.py:164
  69.6 40.1 %copy-start.28 = (f32[1024]{0:T(1024)S(1)}, f32[1024]{0:T(1024)}, u32[]{:S(2)}) copy-start(f32[1024]{0:T(1024)} %param.17) | copy-start | bytes 12292
  69.6 91.9 %all-gather.6.cloned.1.call-start = ((), (), s32[]{:S(2)}) async-start(), calls=%async_computation.13 | async-start | bytes 3276800 | tf_op jit(solution)/shard_map/all_gather | solution.py:173
  109.7 109.8 %copy-start.29 = (f32[320]{0:T(512)}, f32[320]{0:T(512)S(1)}, u32[]{:S(2)}) copy-start(f32[320]{0:T(512)S(1)} %get-tuple-element.91) | copy-start | bytes 3844
  109.7 109.8 %copy-start.34 = (f32[320]{0:T(512)}, f32[320]{0:T(512)S(1)}, u32[]{:S(2)}) copy-start(f32[320]{0:T(512)S(1)} %get-tuple-element.90) | copy-start | bytes 3844
  110.7 106.5 %reduce-scatter.14.cloned.1.call-start = ((), (), s32[]{:S(2)}) async-start(), calls=%async_computation.15 | async-start | bytes 3276800 | tf_op jit(solution)/shard_map/reduce_scatter | solution.py:197
  110.8 10.5 %collective-permute-start = (bf16[320,1024]{1,0:T(8,128)(2,1)}, bf16[320,1024]{1,0:T(8,128)(2,1)}, u32[]{:S(2)}, u32[]{:S(2)}) collective-permute-start(bf16[320,1024]{1,0:T(8,128)(2,1)} %bitcast.100), channel_id=1, source_target_pairs={{0,4},{4,8},{8,12},{12,0},{1,5},{5,9},{9,13},{13,1},{2,6},{6,10},{... | collective-permute-start | bytes 1966088 | tf_op jit(solution)/shard_map/ppermute | solution.py:17
  121.3 26.5 %collective-permute-start.1 = (bf16[320,1024]{1,0:T(8,128)(2,1)}, bf16[320,1024]{1,0:T(8,128)(2,1)}, u32[]{:S(2)}, u32[]{:S(2)}) collective-permute-start(bf16[320,1024]{1,0:T(8,128)(2,1)} %collective-permute-done), channel_id=1, source_target_pairs={{0,4},{4,8},{8,12},{12,0},{1,5},{5,9},{9,13},{13,1},{2,6},{6,10},{... | collective-permute-start | bytes 1966088 | tf_op jit(solution)/shard_map/ppermute | solution.py:17
  122.8 29.8 %collective-permute-start.2 = (bf16[320,1024]{1,0:T(8,128)(2,1)}, bf16[320,1024]{1,0:T(8,128)(2,1)}, u32[]{:S(2)}, u32[]{:S(2)}) collective-permute-start(bf16[320,1024]{1,0:T(8,128)(2,1)} %bitcast.101), channel_id=1, source_target_pairs={{0,12},{4,0},{8,4},{12,8},{1,13},{5,1},{9,5},{13,9},{2,14},{6,2},{... | collective-permute-start | bytes 1966088 | tf_op jit(solution)/shard_map/ppermute | solution.py:19
  123.2 28.6 %copy-start.4 = (bf16[1,320,1024]{2,1,0:T(8,128)(2,1)S(1)}, bf16[1,320,1024]{2,1,0:T(8,128)(2,1)}, u32[]{:S(2)}) copy-start(bf16[1,320,1024]{2,1,0:T(8,128)(2,1)} %param.21) | copy-start | bytes 1966084
  180.9 64.2 %all-gather.8.cloned.1.call-start = ((), (), s32[]{:S(2)}) async-start(), calls=%async_computation.16 | async-start | bytes 1966080 | tf_op jit(solution)/shard_map/all_gather | solution.py:212
  220.7 121.0 %reduce-scatter.20.cloned.1.call-start = ((), (), s32[]{:S(2)}) async-start(), calls=%async_computation.19 | async-start | bytes 1114112 | tf_op jit(solution)/shard_map/reduce_scatter | solution.py:247
  247.6 12.6 %copy-start.10 = (bf16[640,512]{0,1:T(8,128)(2,1)}, bf16[640,512]{0,1:T(8,128)(2,1)S(1)}, u32[]{:S(2)}) copy-start(bf16[640,512]{0,1:T(8,128)(2,1)S(1)} %convolution_convert_fusion.4) | copy-start | bytes 1966084
  247.6 12.6 %slice-start = ((s8[13107200]{0:T(1024)(128)(4,1)}), s8[4194304]{0:T(1024)(128)(4,1)S(1)}, s32[]{:S(2)}) async-start(s8[13107200]{0:T(1024)(128)(4,1)} %bitcast.98), calls=%async_computation.23 | async-start | bytes 8388608
  273.8 82.7 %reduce-scatter.16.cloned.1.call-start = ((), (), s32[]{:S(2)}) async-start(), calls=%async_computation.17 | async-start | bytes 1966080 | tf_op jit(solution)/shard_map/reduce_scatter | solution.py:230
  291.6 106.0 %reduce-scatter.12.cloned.1.call-start = ((), (), s32[]{:S(2)}) async-start(), calls=%async_computation.14 | async-start | bytes 3276800 | tf_op jit(solution)/shard_map/reduce_scatter | solution.py:180
  296.9 167.4 %reduce-scatter.18.cloned.1.call-start = ((), (), s32[]{:S(2)}) async-start(), calls=%async_computation.18 | async-start | bytes 3342336 | tf_op jit(solution)/shard_map/reduce_scatter | solution.py:244
  303.9 236.2 %reduce-scatter.26.cloned.1.call-start = ((), (), s32[]{:S(2)}) async-start(), calls=%async_computation.22 | async-start | bytes 3244032 | tf_op jit(solution)/shard_map/reduce_scatter | solution.py:254
  310.8 305.3 %reduce-scatter.24.cloned.1.call-start = ((), (), s32[]{:S(2)}) async-start(), calls=%async_computation.21 | async-start | bytes 3244032 | tf_op jit(solution)/shard_map/reduce_scatter | solution.py:253
  317.7 374.4 %reduce-scatter.22.cloned.1.call-start = ((), (), s32[]{:S(2)}) async-start(), calls=%async_computation.20 | async-start | bytes 3244032 | tf_op jit(solution)/shard_map/reduce_scatter | solution.py:252
  327.5 28.9 %copy-start.3 = (bf16[1,320,1024]{2,1,0:T(8,128)(2,1)S(1)}, bf16[1,320,1024]{2,1,0:T(8,128)(2,1)}, u32[]{:S(2)}) copy-start(bf16[1,320,1024]{2,1,0:T(8,128)(2,1)} %param.11) | copy-start | bytes 1966084
  327.5 28.9 %copy-start.31 = (f32[1024]{0:T(1024)S(1)}, f32[1024]{0:T(1024)}, u32[]{:S(2)}) copy-start(f32[1024]{0:T(1024)} %param.14) | copy-start | bytes 12292
  327.5 28.9 %copy-start.33 = (f32[320]{0:T(512)S(1)}, f32[320]{0:T(512)}, u32[]{:S(2)}) copy-start(f32[320]{0:T(512)} %copy-done.32) | copy-start | bytes 3844
  339.7 18.3 %copy-start.38 = (f32[1024]{0:T(1024)S(1)}, f32[1024]{0:T(1024)}, u32[]{:S(2)}) copy-start(f32[1024]{0:T(1024)} %get-tuple-element.51) | copy-start | bytes 12292
  339.7 57.9 %copy-start.30 = (f32[320]{0:T(512)S(1)}, f32[320]{0:T(512)}, u32[]{:S(2)}) copy-start(f32[320]{0:T(512)} %copy-done.29) | copy-start | bytes 3844
  339.7 57.9 %copy-start.35 = (f32[320]{0:T(512)S(1)}, f32[320]{0:T(512)}, u32[]{:S(2)}) copy-start(f32[320]{0:T(512)} %copy-done.34) | copy-start | bytes 3844
  339.7 57.9 %copy-start.37 = (f32[320]{0:T(512)S(1)}, f32[320]{0:T(512)}, u32[]{:S(2)}) copy-start(f32[320]{0:T(512)} %copy-done.36) | copy-start | bytes 3844
  339.7 57.9 %copy-start.39 = (f32[320]{0:T(512)S(1)}, f32[320]{0:T(512)}, u32[]{:S(2)}) copy-start(f32[320]{0:T(512)} %get-tuple-element.88) | copy-start | bytes 3844
  397.6 294.5 %copy-start.1 = (bf16[1024,1024]{1,0:T(8,128)(2,1)S(1)}, bf16[1024,1024]{1,0:T(8,128)(2,1)}, u32[]{:S(2)}) copy-start(bf16[1024,1024]{1,0:T(8,128)(2,1)} %param.16) | copy-start | bytes 6291460
  (39 other events, 129.9 us)
Sparse Core Ops, SparseCore 0:
  12.2 30.6 all-gather.3
  69.7 38.1 reduce-scatter.9
  110.8 34.9 all-gather.5
  181.0 36.1 reduce-scatter.13
  220.8 24.2 all-gather.7
  273.9 57.3 reduce-scatter.19
  334.2 22.1 reduce-scatter.15
  358.9 34.8 reduce-scatter.11
  398.1 66.1 reduce-scatter.17
  468.7 71.2 reduce-scatter.25
  544.6 71.4 reduce-scatter.23
  620.5 71.5 reduce-scatter.21
